TPU v7x, 256 devices: a whole 4x4x8 slice. The times are simulated.
256 devices in a mesh: tp: 2 (over z_lo), sp: 32 (over x, y, core), dp: 4 (over z_hi).
Axes of the slice: x: 4, y: 4, z: 8 (z_hi: 4, z_lo: 2; z = z_hi * 2 + z_lo), core: 2. Of those that a mesh axis runs over, the one named last changes fastest.
Arguments:
- queries: bfloat16 [16384, 4096], P(('dp', 'sp'), 'tp'), parts along dimension 0, may hold values from -256 to 256
- key_projection_rows: bfloat16 [16384, 512], P(('dp', 'sp'), 'tp'), parts along dimension 0, may hold values from -8 to 8
- values: bfloat16 [16384, 512], P(('dp', 'sp'), 'tp'), parts along dimension 0, may hold values from -6 to 6
- segment_ids: int32 [16384], P('dp'), parts along dimension 0, may hold values from 0 to 11, never falling along the last dimension, each value on 1 to 1024 neighbouring positions
- residual: bfloat16 [16384, 8192], P(('dp', 'tp'), 'sp'), parts along dimension 0, may hold values from -40 to 40
- out_weight: bfloat16 [4096, 8192], P('tp', 'sp'), may hold values from -0.09375 to 0.09375
- norm_gain: float32 [8192], P('sp'), may hold values from 0.1 to 1.9
- scale_exponent: int32 [8192], P('sp'), may hold values from 7 to 8
Outputs:
- hidden_out: bfloat16 [16384, 8192], P(('dp', 'tp'), 'sp'), parts along dimension 0
- quantized: bfloat16 [16384, 8192], P(('dp', 'tp'), 'sp'), parts along dimension 0
There are 4 independent parts, one for each index of `dp`. A program takes and returns all parts, laid end to end along the dimension named above; an argument that names none is the same for every part. Nothing has to cross between parts.
Inputs may be any that keep to these rules, and one draw needn't show every extreme that they name: `segment_ids`: never falls along the window; every document holds at most a quarter of the window's tokens, and one holds exactly that many.
All inputs are finite; a program needn't handle non-finite values.
Results may differ from a plain program's by a relative error of at most 0.0065.
Values may be sent and summed in bfloat16 or wider, within the bound.
No kernel may reach another device: no remote copies, remote signals or barrier semaphores. Data moves between devices by JAX's collectives and lax.ppermute only.
A program may use at most 64 MiB of HBM per device.

v0:
```python
import jax
import jax.numpy as jnp
from jax import lax
from jax.sharding import PartitionSpec as P

D = 8192
QUERY_HEAD_COUNT = 32
KEY_VALUE_HEADS = 4
HEAD_DIMENSION = 128
epsilon = 1e-05
limit_value = 448.0


def attend_item(query_block, key_block, value_block, query_pos, query_seg, segment_ids, key_pos):
    query_count = query_block.shape[0]
    block_rows = min(512, query_count)
    blocks = query_count // block_rows

    def one_block(packed):
        block_query, block_pos, block_seg = packed
        scores = lax.dot_general(
            block_query, key_block, (((1,), (1,)), ((), ())), preferred_element_type=jnp.float32
        ) * HEAD_DIMENSION ** (-0.5)
        visible = (key_pos[None, :] <= block_pos[:, None]) & (
            segment_ids[None, :] == block_seg[:, None]
        )
        scores = jnp.where(visible, scores, -1e30)
        largest = jnp.max(scores, axis=1, keepdims=True)
        weights = jnp.exp(scores - largest)
        row_total = jnp.sum(weights, axis=1, keepdims=True)
        probabilities = (weights / row_total).astype(jnp.bfloat16)
        return jnp.dot(probabilities, value_block, preferred_element_type=jnp.float32).astype(
            jnp.bfloat16
        )

    results = lax.map(
        one_block,
        (
            query_block.reshape(blocks, block_rows, HEAD_DIMENSION),
            query_pos.reshape(blocks, block_rows),
            query_seg.reshape(blocks, block_rows),
        ),
    )
    return results.reshape(query_count, HEAD_DIMENSION)


def body(
    queries,
    key_projection_rows,
    values,
    segment_ids,
    residual,
    out_weight,
    norm_gain,
    scale_exponent,
):
    sp_count = lax.axis_size("sp")
    token_rows = queries.shape[0]
    half_rows = token_rows // 2
    local_heads = queries.shape[1] // HEAD_DIMENSION
    item_count = 2 * local_heads
    per_device = item_count // sp_count
    window_token_rows = token_rows * sp_count
    query_count = window_token_rows // 2
    group_width = QUERY_HEAD_COUNT // KEY_VALUE_HEADS
    own_index = lax.axis_index("sp")
    query_items = jnp.transpose(
        queries.reshape(2, half_rows, local_heads, HEAD_DIMENSION), (0, 2, 1, 3)
    ).reshape(item_count, half_rows, HEAD_DIMENSION)
    query_recv = lax.all_to_all(query_items, "sp", split_axis=0, concat_axis=1, tiled=True)
    key_all, value_all = (
        lax.all_gather(key_projection_rows, "sp", axis=0, tiled=True),
        lax.all_gather(values, "sp", axis=0, tiled=True),
    )
    key_pos = jnp.arange(window_token_rows, dtype=jnp.int32)
    row_number = jnp.arange(query_count, dtype=jnp.int32)
    source_device = row_number // half_rows
    within = row_number % half_rows
    segment_grid = segment_ids.reshape(sp_count, 2, half_rows)
    number = 0
    item_index = own_index * per_device + number
    which_half = item_index // local_heads
    query_pos = source_device * token_rows + which_half * half_rows + within
    query_seg = lax.dynamic_index_in_dim(segment_grid, which_half, 1, keepdims=False).reshape(
        query_count
    )
    shared_rows = item_index % local_heads // group_width
    key_block = lax.dynamic_slice_in_dim(key_all, shared_rows * HEAD_DIMENSION, HEAD_DIMENSION, 1)
    value_block = lax.dynamic_slice_in_dim(
        value_all, shared_rows * HEAD_DIMENSION, HEAD_DIMENSION, 1
    )
    outputs = [
        attend_item(
            query_recv[number], key_block, value_block, query_pos, query_seg, segment_ids, key_pos
        )
    ]
    own_outputs = jnp.stack(outputs)
    column_count = out_weight.shape[1]
    start_sum = jnp.zeros((sp_count, 2, half_rows, column_count), jnp.float32)
    pieces = lax.all_gather(own_outputs, "sp", axis=0, tiled=True)

    def add_one(number, current):
        head_number = number % local_heads
        which_half = number // local_heads
        head_weight = lax.dynamic_slice_in_dim(
            out_weight, head_number * HEAD_DIMENSION, HEAD_DIMENSION, 0
        )
        chosen = lax.dynamic_index_in_dim(pieces, number, 0, keepdims=False)
        product_term = jnp.dot(chosen, head_weight, preferred_element_type=jnp.float32).reshape(
            sp_count, 1, half_rows, column_count
        )
        corner = (0, which_half, 0, 0)
        earlier = lax.dynamic_slice(current, corner, (sp_count, 1, half_rows, column_count))
        return lax.dynamic_update_slice(current, earlier + product_term, corner)

    combined = lax.fori_loop(0, pieces.shape[0], add_one, start_sum)
    flattened = combined.reshape(window_token_rows, column_count)
    share_rows = window_token_rows // lax.axis_size("tp")
    whole_sum = lax.psum(flattened, "tp")
    summed = lax.dynamic_slice_in_dim(whole_sum, lax.axis_index("tp") * share_rows, share_rows, 0)
    projected = summed.astype(jnp.bfloat16)
    hidden_out = (residual.astype(jnp.float32) + projected.astype(jnp.float32)).astype(jnp.bfloat16)
    widened = hidden_out.astype(jnp.float32)
    square_sum = lax.psum(jnp.sum(widened * widened, axis=1), "sp")
    mean_square = (square_sum / D)[:, None]
    normed = widened * lax.rsqrt(mean_square + epsilon) * norm_gain[None, :]
    clip_bound = (limit_value * jnp.exp2(-scale_exponent.astype(jnp.float32)))[None, :]
    quantized = jnp.clip(normed, -clip_bound, clip_bound).astype(jnp.bfloat16)
    return (hidden_out, quantized)


def solution(mesh):
    in_specs = (
        P(("dp", "sp"), "tp"),
        P(("dp", "sp"), "tp"),
        P(("dp", "sp"), "tp"),
        P("dp"),
        P(("dp", "tp"), "sp"),
        P("tp", "sp"),
        P("sp"),
        P("sp"),
    )
    out_specs = (P(("dp", "tp"), "sp"), P(("dp", "tp"), "sp"))
    return jax.shard_map(body, mesh=mesh, in_specs=in_specs, out_specs=out_specs, check_vma=False)
```

profile of v0, /device:TPU:1, one launch (start us, length us, event | category | flops | bytes accessed | tf_op | source)
XLA Modules:
  0.0 569.2 jit_solution(7606608849317972235)
XLA Ops:
  10.8 8.6 %all-to-all-start = ((bf16[32,64,128]{2,1,0:T(8,128)(2,1)}), bf16[32,64,128]{2,1,0:T(8,128)(2,1)S(1)}, u32[]{:S(2)}, u32[]{:S(2)}) async-start(bf16[32,64,128]{2,1,0:T(8,128)(2,1)} %bitcast.4), calls=%async_computation | async-start | bytes 1048576 | tf_op jit(solution)/shard_map/all_to_all | solution.py:70
  19.8 43.6 %all-gather.6.cloned.1.call-done = bf16[4096,256]{1,0:T(8,128)(2,1)} async-done(((bf16[128,256]{1,0:T(8,128)(2,1)}), bf16[4096,256]{1,0:T(8,128)(2,1)}) %all-gather.6.cloned.1.call-update) | async-done | bytes 2097168 | tf_op jit(solution)/shard_map/all_gather | solution.py:73
  64.6 49.3 %all-gather.4.cloned.1.call-done = bf16[4096,256]{1,0:T(8,128)(2,1)} async-done(((bf16[128,256]{1,0:T(8,128)(2,1)}), bf16[4096,256]{1,0:T(8,128)(2,1)}) %all-gather.4.cloned.1.call-update) | async-done | bytes 2097168 | tf_op jit(solution)/shard_map/all_gather | solution.py:72
  115.2 24.3 %while.27 = (s32[]{:T(128)}, bf16[4,512,128]{2,1,0:T(8,128)(2,1)S(1)}, s32[4,512]{1,0:T(4,128)S(1)}, s32[4096]{0:T(1024)S(1)}, s32[4,512]{1,0:T(4,128)S(1)}, /*i...) while((s32[]{:T(128)}, ...), condition=%wide.region_3.4_spmd.clone, body=%wide.region_0.3_spmd.clone.sunk | while | flops 1096875008 | bytes 27564136 | solution.py:36
  140.3 77.1 %all-gather.8.cloned.1.call-done = bf16[32,2048,128]{2,1,0:T(8,128)(2,1)} async-done(((bf16[1,2048,128]{2,1,0:T(8,128)(2,1)}), bf16[32,2048,128]{2,1,0:T(8,128)(2,1)}) %all-gather.8.cloned.1.call-update) | async-done | bytes 16777232 | tf_op jit(solution)/shard_map/all_gather | solution.py:100
  219.9 174.8 %while.26 = (s32[]{:T(128)}, f32[32,2,64,256]{3,2,1,0:T(8,128)}, bf16[32,2048,128]{2,1,0:T(8,128)(2,1)}, bf16[2048,256]{1,0:T(8,128)(2,1)}, s32[]{:T(128)}, /*in...) while((s32[]{:T(128)}, f32[32,2,64,256]{3,2,1,0:T(8,128)}, ...), condition=%wide.region_5.6_spmd, body=%wide.region_4.5_spmd.sunk | while | flops 134742032 | bytes 10027344 | solution.py:116
  222.7 2.6 bitcast_dynamic-update-slice_fusion.2
  233.6 2.6 bitcast_dynamic-update-slice_fusion.2
  244.4 2.6 bitcast_dynamic-update-slice_fusion.2
  255.3 2.6 bitcast_dynamic-update-slice_fusion.2
  260.7 2.6 bitcast_dynamic-update-slice_fusion.2
  282.4 2.6 bitcast_dynamic-update-slice_fusion.2
  287.9 2.6 bitcast_dynamic-update-slice_fusion.2
  298.7 2.6 bitcast_dynamic-update-slice_fusion.2
  309.6 2.6 bitcast_dynamic-update-slice_fusion.2
  315.1 2.6 bitcast_dynamic-update-slice_fusion.2
  320.6 2.6 bitcast_dynamic-update-slice_fusion.2
  326.0 2.6 bitcast_dynamic-update-slice_fusion.2
  331.5 2.6 bitcast_dynamic-update-slice_fusion.2
  337.0 2.6 bitcast_dynamic-update-slice_fusion.2
  342.5 2.6 bitcast_dynamic-update-slice_fusion.2
  348.0 2.6 bitcast_dynamic-update-slice_fusion.2
  353.5 2.6 bitcast_dynamic-update-slice_fusion.2
  359.0 2.6 bitcast_dynamic-update-slice_fusion.2
  364.5 2.6 bitcast_dynamic-update-slice_fusion.2
  370.0 2.6 bitcast_dynamic-update-slice_fusion.2
  375.5 2.6 bitcast_dynamic-update-slice_fusion.2
  381.0 2.6 bitcast_dynamic-update-slice_fusion.2
  386.5 2.6 bitcast_dynamic-update-slice_fusion.2
  392.0 2.6 bitcast_dynamic-update-slice_fusion.2
  394.7 100.2 %all-reduce.1 = bf16[4096,256]{1,0:T(8,128)(2,1)S(1)} all-reduce(f32[4096,256]{1,0:T(8,128)} %bitcast.61), channel_id=1, replica_groups=mesh['tp'=2,'sp'=32,'dp'=4] {'tp'}, use_global_device_ids=true, to_apply=%region_6.7 | all-reduce | flops 1048576 | bytes 6291456 | tf_op jit(solution)/shard_map/psum | solution.py:119
  496.6 64.7 %psum.15 = f32[2048]{0:T(1024)S(1)} all-reduce(f32[2048]{0:T(1024)S(1)} %get-tuple-element.206), channel_id=1, replica_groups=mesh['tp'=2,'sp'=32,'dp'=4] {'sp'}, use_global_device_ids=true, to_apply=%region_8.9 | all-reduce | flops 2048 | bytes 16384 | tf_op jit(solution)/shard_map/psum | solution.py:124
  (120 shorter events, 148.3 us)
Async XLA Ops:
  7.2 12.3 %copy-start.2 = (s32[4096]{0:T(1024)S(1)}, s32[4096]{0:T(1024)}, u32[]{:S(2)}) copy-start(s32[4096]{0:T(1024)} %param.15) | copy-start | bytes 49156
  7.2 56.2 %all-gather.6.cloned.1.call-start = ((), (), s32[]{:S(2)}) async-start(), calls=%async_computation.2 | async-start | bytes 2162688 | tf_op jit(solution)/shard_map/all_gather | solution.py:73
  7.9 106.0 %all-gather.4.cloned.1.call-start = ((), (), s32[]{:S(2)}) async-start(), calls=%async_computation.1 | async-start | bytes 2162688 | tf_op jit(solution)/shard_map/all_gather | solution.py:72
  10.8 104.4 %all-to-all-start = ((bf16[32,64,128]{2,1,0:T(8,128)(2,1)}), bf16[32,64,128]{2,1,0:T(8,128)(2,1)S(1)}, u32[]{:S(2)}, u32[]{:S(2)}) async-start(bf16[32,64,128]{2,1,0:T(8,128)(2,1)} %bitcast.4), calls=%async_computation | async-start | bytes 1048576 | tf_op jit(solution)/shard_map/all_to_all | solution.py:70
  19.4 198.0 %all-gather.8.cloned.1.call-start = ((), (), s32[]{:S(2)}) async-start(), calls=%async_computation.3 | async-start | bytes 17301504 | tf_op jit(solution)/shard_map/all_gather | solution.py:100
  115.2 25.1 %copy-start.4 = (s32[256]{0:T(256)S(1)}, s32[256]{0:T(256)}, u32[]{:S(2)}) copy-start(s32[256]{0:T(256)} %param.19) | copy-start | bytes 3076
  139.5 0.8 copy-start.1
  394.7 166.6 %copy-start.3 = (f32[256]{0:T(256)S(1)}, f32[256]{0:T(256)}, u32[]{:S(2)}) copy-start(f32[256]{0:T(256)} %param.18) | copy-start | bytes 3076
  496.5 66.2 %copy-start = (bf16[2048,256]{1,0:T(8,128)(2,1)}, bf16[2048,256]{1,0:T(8,128)(2,1)S(1)}, u32[]{:S(2)}) copy-start(bf16[2048,256]{1,0:T(8,128)(2,1)S(1)} %get-tuple-element.207) | copy-start | bytes 3145732
Sparse Core Ops, SparseCore 0:
  10.5 52.7 all-gather.5
  65.9 47.9 all-gather.3
  140.4 76.9 all-gather.7
where the time goes:
time: 574 us; the launch traced here: 569 us
  waiting for transfers between devices  171 us (30%)
  blocking collectives  165 us (29%)
  matrix products  103 us (18%)
  local copies, waits for them, and re-layouts  98.9 us (17%)
  between operations  14 us (2%)
  starting transfers between devices  8.69 us (2%)
  other arithmetic  8.28 us (1%)
    psum x1, blocking collectives, body(): whole_sum = lax.psum(flattened, 'tp')  100 us
    dot_general x32, matrix products, add_one(): jnp.dot(chosen, head_weight, preferred_element_type=jnp.float32)  83.6 us
    all_gather x1, waiting for transfers between devices, body(): pieces = lax.all_gather(own_outputs, 'sp', axis=0, tiled=True)  77.1 us
    psum x1, blocking collectives, body(): square_sum = lax.psum(jnp.sum(widened * widened, axis=1), 'sp')  64.7 us
    dynamic_slice x32, local copies, waits for them, and re-layouts, add_one(): lax.dynamic_slice(current, corner, (sp_count, 1, half_rows, column_count))  56.2 us
    all_gather x1, waiting for transfers between devices, body(): lax.all_gather(key_projection_rows, 'sp', axis=0, tiled=True)  49.3 us
    all_gather x1, waiting for transfers between devices, body(): lax.all_gather(values, 'sp', axis=0, tiled=True)  43.6 us
    dynamic_slice x32, local copies, waits for them, and re-layouts, add_one(): chosen = lax.dynamic_index_in_dim(pieces, number, 0, keepdims=False)  34.6 us
  transfers between devices with their start and end apart: 4, of which 3 were waited for; matrix products, arithmetic and copies ran while one was open for 1% of the time, Pallas kernels for 0%

commit v1 on v0

--- a/solution.py
+++ b/solution.py
@@ -9,6 +9,16 @@
 HEAD_DIMENSION = 128
 epsilon = 1e-05
 limit_value = 448.0
+
+
+def advance_the_slices(arr_in, named_axis, axis_no):
+    block_list = []
+    for _ in range(lax.axis_size(named_axis)):
+        block_list.append(arr_in)
+    return jnp.concatenate(
+        lax.all_to_all(jnp.stack(block_list, axis=0), named_axis, split_axis=0, concat_axis=0),
+        axis=axis_no,
+    )
 
 
 def attend_item(query_block, key_block, value_block, query_pos, query_seg, segment_ids, key_pos):
@@ -69,7 +79,7 @@
     ).reshape(item_count, half_rows, HEAD_DIMENSION)
     query_recv = lax.all_to_all(query_items, "sp", split_axis=0, concat_axis=1, tiled=True)
     key_all, value_all = (
-        lax.all_gather(key_projection_rows, "sp", axis=0, tiled=True),
+        advance_the_slices(key_projection_rows, "sp", 0),
         lax.all_gather(values, "sp", axis=0, tiled=True),
     )
     key_pos = jnp.arange(window_token_rows, dtype=jnp.int32)

time: 574 us -> 542 us (0.944)
  waiting for transfers between devices: 171 us -> 127 us
  matrix products: 103 us -> 110 us
    all_gather x1 -> x0, waiting for transfers between devices: 49.3 us -> none  [body(): lax.all_gather(key_projection_rows, 'sp', axis=0, tiled=True)]
    all_to_all x0 -> x1, waiting for transfers between devices: none -> 27.8 us  [advance_the_slices(): lax.all_to_all(jnp.stack(block_list, axis=0), named_axis, split_axis=0, c...]
    all_gather x1, waiting for transfers between devices: 43.6 us -> 20 us  [body(): lax.all_gather(values, 'sp', axis=0, tiled=True)]
    all_to_all x0 -> x1, starting transfers between devices: none -> 8.58 us  [advance_the_slices(): lax.all_to_all(jnp.stack(block_list, axis=0), named_axis, split_axis=0, c...]
where the time goes in v1:
time: 542 us; the launch traced here: 537 us
  blocking collectives  165 us (30%)
  waiting for transfers between devices  127 us (23%)
  matrix products  110 us (20%)
  local copies, waits for them, and re-layouts  98.3 us (18%)
  between operations  14.3 us (3%)
  starting transfers between devices  13.7 us (3%)
  other arithmetic  8.25 us (2%)
    psum x1, blocking collectives, body(): whole_sum = lax.psum(flattened, 'tp')  100 us
    dot_general x32, matrix products, add_one(): jnp.dot(chosen, head_weight, preferred_element_type=jnp.float32)  84.7 us
    all_gather x1, waiting for transfers between devices, body(): pieces = lax.all_gather(own_outputs, 'sp', axis=0, tiled=True)  78.5 us
    psum x1, blocking collectives, body(): square_sum = lax.psum(jnp.sum(widened * widened, axis=1), 'sp')  64.7 us
    dynamic_slice x32, local copies, waits for them, and re-layouts, add_one(): lax.dynamic_slice(current, corner, (sp_count, 1, half_rows, column_count))  56.2 us
    dynamic_slice x32, local copies, waits for them, and re-layouts, add_one(): chosen = lax.dynamic_index_in_dim(pieces, number, 0, keepdims=False)  34.6 us
    all_to_all x1, waiting for transfers between devices, advance_the_slices(): lax.all_to_all(jnp.stack(block_list, axis=0), named_axis, split_axis=0, c...  27.8 us
    all_gather x1, waiting for transfers between devices, body(): lax.all_gather(values, 'sp', axis=0, tiled=True)  20 us
  transfers between devices with their start and end apart: 4, of which 3 were waited for; matrix products, arithmetic and copies ran while one was open for 1% of the time, Pallas kernels for 0%

profile of v1, /device:TPU:1, one launch (start us, length us, event | category | flops | bytes accessed | tf_op | source)
XLA Modules:
  0.0 537.4 jit_solution(6444248883934384883)
XLA Ops:
  10.3 8.6 %all-to-all-start.1 = ((bf16[32,128,256]{2,1,0:T(8,128)(2,1)}), bf16[32,128,256]{2,1,0:T(8,128)(2,1)S(1)}, u32[]{:S(2)}, u32[]{:S(2)}) async-start(bf16[32,128,256]{2,1,0:T(8,128)(2,1)} %stack.2), calls=%async_computation.1 | async-start | bytes 4194304 | tf_op jit(solution)/shard_map/all_to_all | solution.py:19
  20.3 27.8 %all-to-all-done.1 = bf16[32,128,256]{2,1,0:T(8,128)(2,1)S(1)} async-done(((bf16[32,128,256]{2,1,0:T(8,128)(2,1)}), bf16[32,128,256]{2,1,0:T(8,128)(2,1)S(1)}, u32[]{:S(2)}, u32[]{:S(2)}) %all-to-all-start.1) | async-done | bytes 2097184 | tf_op jit(solution)/shard_map/all_to_all | solution.py:19
  48.2 5.0 all-to-all-start
  53.3 20.0 %all-gather.3.cloned.1.call-done = bf16[4096,256]{1,0:T(8,128)(2,1)} async-done(((bf16[128,256]{1,0:T(8,128)(2,1)}), bf16[4096,256]{1,0:T(8,128)(2,1)}) %all-gather.3.cloned.1.call-update) | async-done | bytes 2097168 | tf_op jit(solution)/shard_map/all_gather | solution.py:83
  74.7 31.0 %while.27 = (s32[]{:T(128)}, bf16[4,512,128]{2,1,0:T(8,128)(2,1)}, s32[4,512]{1,0:T(4,128)S(1)}, s32[4096]{0:T(1024)S(1)}, s32[4,512]{1,0:T(4,128)S(1)}, /*index...) while((s32[]{:T(128)}, bf16[4,512,128]{2,1,0:T(8,128)(2,1)}, ...), condition=%wide.region_3.4_spmd.clone, body=%wide.region_0.3_spmd.clone.sunk | while | flops 1096875008 | bytes 27565152 | solution.py:46
  74.7 3.6 fusion.40
  79.6 2.8 fusion.42
  82.4 3.6 fusion.40
  87.3 2.8 fusion.42
  90.2 3.6 fusion.40
  95.1 2.8 fusion.42
  97.9 3.6 fusion.40
  102.8 2.8 fusion.42
  105.7 78.5 %all-gather.5.cloned.1.call-done = bf16[32,2048,128]{2,1,0:T(8,128)(2,1)} async-done(((bf16[1,2048,128]{2,1,0:T(8,128)(2,1)}), bf16[32,2048,128]{2,1,0:T(8,128)(2,1)}) %all-gather.5.cloned.1.call-update) | async-done | bytes 16777232 | tf_op jit(solution)/shard_map/all_gather | solution.py:110
  186.6 175.9 %while.26 = (s32[]{:T(128)}, f32[32,2,64,256]{3,2,1,0:T(8,128)}, bf16[32,2048,128]{2,1,0:T(8,128)(2,1)}, bf16[2048,256]{1,0:T(8,128)(2,1)}, s32[]{:T(128)}, /*in...) while((s32[]{:T(128)}, f32[32,2,64,256]{3,2,1,0:T(8,128)}, ...), condition=%wide.region_5.6_spmd, body=%wide.region_4.5_spmd.sunk | while | flops 134742032 | bytes 10027344 | solution.py:126
  195.0 2.6 bitcast_dynamic-update-slice_fusion.2
  277.4 2.6 bitcast_dynamic-update-slice_fusion.2
  293.9 2.6 bitcast_dynamic-update-slice_fusion.2
  299.4 2.6 bitcast_dynamic-update-slice_fusion.2
  304.9 2.6 bitcast_dynamic-update-slice_fusion.2
  310.4 2.6 bitcast_dynamic-update-slice_fusion.2
  315.9 2.6 bitcast_dynamic-update-slice_fusion.2
  321.4 2.6 bitcast_dynamic-update-slice_fusion.2
  326.9 2.6 bitcast_dynamic-update-slice_fusion.2
  332.4 2.6 bitcast_dynamic-update-slice_fusion.2
  337.9 2.6 bitcast_dynamic-update-slice_fusion.2
  343.4 2.6 bitcast_dynamic-update-slice_fusion.2
  348.9 2.6 bitcast_dynamic-update-slice_fusion.2
  354.4 2.6 bitcast_dynamic-update-slice_fusion.2
  359.9 2.6 bitcast_dynamic-update-slice_fusion.2
  362.5 100.2 %all-reduce.1 = bf16[4096,256]{1,0:T(8,128)(2,1)S(1)} all-reduce(f32[4096,256]{1,0:T(8,128)} %bitcast.62), channel_id=1, replica_groups=mesh['tp'=2,'sp'=32,'dp'=4] {'tp'}, use_global_device_ids=true, to_apply=%region_6.7 | all-reduce | flops 1048576 | bytes 6291456 | tf_op jit(solution)/shard_map/psum | solution.py:129
  464.4 64.7 %psum.15 = f32[2048]{0:T(1024)S(1)} all-reduce(f32[2048]{0:T(1024)S(1)} %get-tuple-element.206), channel_id=1, replica_groups=mesh['tp'=2,'sp'=32,'dp'=4] {'sp'}, use_global_device_ids=true, to_apply=%region_8.9 | all-reduce | flops 2048 | bytes 16384 | tf_op jit(solution)/shard_map/psum | solution.py:134
  (120 shorter events, 152.2 us)
Async XLA Ops:
  7.2 11.8 %copy-start.2 = (s32[4096]{0:T(1024)S(1)}, s32[4096]{0:T(1024)}, u32[]{:S(2)}) copy-start(s32[4096]{0:T(1024)} %param.15) | copy-start | bytes 49156
  7.2 12.0 %copy-start.1 = (bf16[128,2048]{1,0:T(8,128)(2,1)S(1)}, bf16[128,2048]{1,0:T(8,128)(2,1)}, u32[]{:S(2)}) copy-start(bf16[128,2048]{1,0:T(8,128)(2,1)} %param.12) | copy-start | bytes 1572868
  7.2 66.2 %all-gather.3.cloned.1.call-start = ((), (), s32[]{:S(2)}) async-start(), calls=%async_computation.2 | async-start | bytes 2162688 | tf_op jit(solution)/shard_map/all_gather | solution.py:83
  10.3 37.9 %all-to-all-start.1 = ((bf16[32,128,256]{2,1,0:T(8,128)(2,1)}), bf16[32,128,256]{2,1,0:T(8,128)(2,1)S(1)}, u32[]{:S(2)}, u32[]{:S(2)}) async-start(bf16[32,128,256]{2,1,0:T(8,128)(2,1)} %stack.2), calls=%async_computation.1 | async-start | bytes 4194304 | tf_op jit(solution)/shard_map/all_to_all | solution.py:19
  48.2 26.5 %all-to-all-start = ((bf16[32,64,128]{2,1,0:T(8,128)(2,1)}), bf16[32,64,128]{2,1,0:T(8,128)(2,1)}, u32[]{:S(2)}, u32[]{:S(2)}) async-start(bf16[32,64,128]{2,1,0:T(8,128)(2,1)} %bitcast.4), calls=%async_computation | async-start | bytes 1048576 | tf_op jit(solution)/shard_map/all_to_all | solution.py:80
  53.2 131.0 %all-gather.5.cloned.1.call-start = ((), (), s32[]{:S(2)}) async-start(), calls=%async_computation.3 | async-start | bytes 17301504 | tf_op jit(solution)/shard_map/all_gather | solution.py:110
  74.7 31.0 %copy-start.4 = (s32[256]{0:T(256)S(1)}, s32[256]{0:T(256)}, u32[]{:S(2)}) copy-start(s32[256]{0:T(256)} %param.19) | copy-start | bytes 3076
  362.5 166.6 %copy-start.3 = (f32[256]{0:T(256)S(1)}, f32[256]{0:T(256)}, u32[]{:S(2)}) copy-start(f32[256]{0:T(256)} %param.18) | copy-start | bytes 3076
  464.4 66.2 %copy-start = (bf16[2048,256]{1,0:T(8,128)(2,1)}, bf16[2048,256]{1,0:T(8,128)(2,1)S(1)}, u32[]{:S(2)}) copy-start(bf16[2048,256]{1,0:T(8,128)(2,1)S(1)} %get-tuple-element.207) | copy-start | bytes 3145732
Sparse Core Ops, SparseCore 0:
  10.5 62.7 all-gather.2
  105.8 78.3 all-gather.4
